TPU v7x, 32 devices: a whole 2x2x4 slice. The times are simulated.
32 devices in a mesh: row: 4 (over y, core), col: 8 (over z, x).
Axes of the slice: x: 2, y: 2, z: 4, core: 2. Of those that a mesh axis runs over, the one named last changes fastest.
Arguments:
- pixels: bfloat16 [128, 256, 588], P('row', 'col'), may hold values from -6 to 6
- text: bfloat16 [12288, 1024], P(('row', 'col')), may hold values from -6 to 6
- token_source: int32 [36864], P(('row', 'col')), may hold values from 0 to 1407, as said below
- example_ids: int32 [36864], P(('row', 'col')), may hold values from 0 to 95, as said below
- cotangent: bfloat16 [36864, 1024], P(('row', 'col')), may hold values from -6 to 6
- conv_weight: bfloat16 [588, 1664], P(None, ('row', 'col')), may hold values from -0.25 to 0.25
- conv_bias: bfloat16 [1664], P(('row', 'col')), may hold values from -3 to 3
- proj_weight: bfloat16 [1664, 1024], P(None, ('row', 'col')), may hold values from -0.15625 to 0.15625
- proj_bias: bfloat16 [1024], P(('row', 'col')), may hold values from -3 to 3
- first_gain: bfloat16 [1024], P(('row', 'col')), may hold values from 0.099609375 to 1.8984375
- query_weight: bfloat16 [1024, 1024], P(('row', 'col')), may hold values from -0.1875 to 0.1875
- key_weight: bfloat16 [1024, 1024], P(('row', 'col')), may hold values from -0.1875 to 0.1875
- value_weight: bfloat16 [1024, 1024], P(('row', 'col')), may hold values from -0.1875 to 0.1875
- out_weight: bfloat16 [1024, 1024], P(None, ('row', 'col')), may hold values from -3 to 3
- second_gain: bfloat16 [1024], P(('row', 'col')), may hold values from 0.099609375 to 1.8984375
- gate_weight: bfloat16 [1024, 2816], P(('row', 'col')), may hold values from -0.1875 to 0.1875
- up_weight: bfloat16 [1024, 2816], P(('row', 'col')), may hold values from -0.1875 to 0.1875
- down_weight: bfloat16 [2816, 1024], P(None, ('row', 'col')), may hold values from -0.109375 to 0.109375
Outputs:
- output: bfloat16 [36864, 1024], P(('row', 'col'))
- pixel_grad: float32 [128, 256, 588], P('row', 'col')
- conv_weight_grad: float32 [588, 1664], P(None, ('row', 'col'))
- conv_bias_grad: float32 [1664], P(('row', 'col'))
- proj_weight_grad: float32 [1664, 1024], P(None, ('row', 'col'))
- proj_bias_grad: float32 [1024], P(('row', 'col'))
- first_gain_grad: float32 [1024], P(('row', 'col'))
- query_grad: float32 [1024, 1024], P(('row', 'col'))
- key_grad: float32 [1024, 1024], P(('row', 'col'))
- value_grad: float32 [1024, 1024], P(('row', 'col'))
- out_grad: float32 [1024, 1024], P(None, ('row', 'col'))
- second_gain_grad: float32 [1024], P(('row', 'col'))
- gate_grad: float32 [1024, 2816], P(('row', 'col'))
- up_grad: float32 [1024, 2816], P(('row', 'col'))
- down_grad: float32 [2816, 1024], P(None, ('row', 'col'))
Inputs may be any that keep to these rules, and one draw needn't show every extreme that they name: `token_source`: within each packed row (tokens t with the same t div 1152) the sources are distinct; a row takes either all 1024 patch slots and text slots 1024 to 1151, or three quarters of its patch slots and all 384 text slots; slots that no token names are empty. `example_ids`: A packed row holds one example of 1152 tokens or three of 384 tokens each, every example contiguous and within one row; ids of different examples differ.
All inputs are finite; a program needn't handle non-finite values.
Results may differ from a plain program's by a relative error of at most 0.015.
Values may be sent and summed in bfloat16 or wider, within the bound.
No kernel may reach another device: no remote copies, remote signals or barrier semaphores. Data moves between devices by JAX's collectives and lax.ppermute only.
A program may use at most 256 MiB of HBM per device.

v0:
```python
import jax
import jax.numpy as jnp
from jax import lax
from jax.sharding import PartitionSpec as P

D = 1024
H = 16
HD = 64
PATCH_SLOTS = 1024
TEXT = 128
ROW = 1152


def normed(values, gain):
    return values * lax.rsqrt(jnp.mean(values * values, axis=-1, keepdims=True) + 1e-06) * gain


def gelu_tanh(values):
    return jax.nn.gelu(values, approximate=True)


def matmul(left, right):
    return jnp.dot(left, right, preferred_element_type=jnp.float32)


def left_contract(left, right):
    return lax.dot_general(
        left, right, (((0,), (0,)), ((), ())), preferred_element_type=jnp.float32
    )


def right_contract(left, right):
    return lax.dot_general(
        left, right, (((1,), (1,)), ((), ())), preferred_element_type=jnp.float32
    )


def split_heads(values):
    return values.reshape(values.shape[0], H, HD).transpose(1, 0, 2)


def merge_heads(values):
    return values.transpose(1, 0, 2).reshape(values.shape[1], H * HD)


def masked_scores(query, keys, same_example):
    return jnp.where(same_example, right_contract(query, keys) * 0.125, -1000000000.0)


def attend_row(parts):
    queries, keys_all, values_all, example_row = parts
    same_example = example_row[:, None] == example_row[None, :]

    def one_head(pieces):
        query, keys, values = pieces
        scores = masked_scores(query, keys, same_example)
        row_max = jnp.max(scores, axis=-1, keepdims=True)
        powers = jnp.exp(scores - row_max)
        totals = jnp.sum(powers, axis=-1, keepdims=True)
        chances = (powers / totals).astype(jnp.bfloat16)
        return (matmul(chances, values), (row_max + jnp.log(totals))[:, 0])

    outputs, logsum = lax.map(
        one_head, (split_heads(queries), split_heads(keys_all), split_heads(values_all))
    )
    return (merge_heads(outputs), logsum)


def attend_back(parts):
    queries, keys_all, values_all, grads_all, logsum, example_row = parts
    same_example = example_row[:, None] == example_row[None, :]

    def one_head(pieces):
        query, keys, values, grads, logs = pieces
        scores = masked_scores(query, keys, same_example)
        chances = jnp.exp(scores - logs[:, None])
        grad_chances = right_contract(grads, values)
        deltas = jnp.sum(chances * grad_chances, axis=-1, keepdims=True)
        grad_scores = (chances * (grad_chances - deltas)).astype(jnp.bfloat16)
        return (
            matmul(grad_scores, keys) * 0.125,
            left_contract(grad_scores, query) * 0.125,
            left_contract(chances.astype(jnp.bfloat16), grads),
        )

    grad_query, grad_keys, grad_values = lax.map(
        one_head,
        (
            split_heads(queries),
            split_heads(keys_all),
            split_heads(values_all),
            split_heads(grads_all),
            logsum,
        ),
    )
    return (merge_heads(grad_query), merge_heads(grad_keys), merge_heads(grad_values))


def shards(
    pixels,
    text,
    token_source,
    example_ids,
    cotangent,
    conv_weight,
    conv_bias,
    proj_weight,
    proj_bias,
    first_gain,
    query_weight,
    key_weight,
    value_weight,
    out_weight,
    second_gain,
    gate_weight,
    up_weight,
    down_weight,
):
    (
        conv_whole,
        conv_add,
        proj_whole,
        proj_add,
        gain_one,
        query_whole,
        key_whole,
        value_whole,
        out_whole,
        gain_two,
    ) = (
        lax.all_gather(conv_weight, ("row", "col"), axis=1, tiled=True),
        lax.all_gather(conv_bias, ("row", "col"), axis=0, tiled=True),
        lax.all_gather(proj_weight, ("row", "col"), axis=1, tiled=True),
        lax.all_gather(proj_bias, ("row", "col"), axis=0, tiled=True),
        lax.all_gather(first_gain, ("row", "col"), axis=0, tiled=True),
        lax.all_gather(query_weight, ("row", "col"), axis=0, tiled=True),
        lax.all_gather(key_weight, ("row", "col"), axis=0, tiled=True),
        lax.all_gather(value_weight, ("row", "col"), axis=0, tiled=True),
        lax.all_gather(out_weight, ("row", "col"), axis=1, tiled=True),
        lax.all_gather(second_gain, ("row", "col"), axis=0, tiled=True),
    )
    gate_whole, up_whole, down_whole = (
        lax.all_gather(gate_weight, ("row", "col"), axis=0, tiled=True),
        lax.all_gather(up_weight, ("row", "col"), axis=0, tiled=True),
        lax.all_gather(down_weight, ("row", "col"), axis=1, tiled=True),
    )
    patch_rows = pixels.reshape(-1, pixels.shape[-1])
    visual = (matmul(patch_rows, conv_whole) + conv_add.astype(jnp.float32)).astype(jnp.bfloat16)
    embedded = (matmul(visual, proj_whole) + proj_add.astype(jnp.float32)).astype(jnp.bfloat16)
    arrived = lax.all_to_all(embedded, ("row", "col"), split_axis=0, concat_axis=0, tiled=True)
    row_total = token_source.shape[0] // ROW
    pooled = jnp.concatenate(
        (arrived.reshape(row_total, PATCH_SLOTS, D), text.reshape(row_total, 3 * TEXT, D)), axis=1
    )
    sources = token_source.reshape(row_total, ROW)
    example_rows = example_ids.reshape(row_total, ROW)
    residual = (
        jax.vmap(lambda pooled_row, chosen: pooled_row[chosen])(pooled, sources)
        .reshape(-1, D)
        .astype(jnp.float32)
    )

    def by_rows(values):
        return values.reshape(row_total, ROW, values.shape[-1])

    gain_first = gain_one.astype(jnp.float32)
    gain_second = gain_two.astype(jnp.float32)
    normal_in = normed(residual, gain_first).astype(jnp.bfloat16)
    queries = matmul(normal_in, query_whole).astype(jnp.bfloat16)
    keys_all = matmul(normal_in, key_whole).astype(jnp.bfloat16)
    values_all = matmul(normal_in, value_whole).astype(jnp.bfloat16)
    attended, logsum = lax.map(
        attend_row, (by_rows(queries), by_rows(keys_all), by_rows(values_all), example_rows)
    )
    mixed = attended.reshape(-1, D).astype(jnp.bfloat16)
    middle = residual + matmul(mixed, out_whole)
    normal_mid = normed(middle, gain_second).astype(jnp.bfloat16)
    gate = matmul(normal_mid, gate_whole)
    upward = matmul(normal_mid, up_whole)
    gate_act = gelu_tanh(gate)
    hidden = (gate_act * upward).astype(jnp.bfloat16)
    output = (middle + matmul(hidden, down_whole)).astype(jnp.bfloat16)
    gate_whole, up_whole, down_whole = (
        lax.all_gather(gate_weight, ("row", "col"), axis=0, tiled=True),
        lax.all_gather(up_weight, ("row", "col"), axis=0, tiled=True),
        lax.all_gather(down_weight, ("row", "col"), axis=1, tiled=True),
    )
    grad_down = left_contract(hidden, cotangent)
    grad_hidden = right_contract(cotangent, down_whole)
    gelu_pull = jax.vjp(gelu_tanh, gate)[1]
    grad_gate = gelu_pull(grad_hidden * upward)[0].astype(jnp.bfloat16)
    grad_upward = (grad_hidden * gate_act).astype(jnp.bfloat16)
    ffn_sums = (
        lax.psum_scatter(
            left_contract(normal_mid, grad_gate), ("row", "col"), scatter_dimension=0, tiled=True
        ),
        lax.psum_scatter(
            left_contract(normal_mid, grad_upward), ("row", "col"), scatter_dimension=0, tiled=True
        ),
        lax.psum_scatter(grad_down, ("row", "col"), scatter_dimension=1, tiled=True),
    )
    grad_normal_mid = right_contract(grad_gate, gate_whole) + right_contract(grad_upward, up_whole)
    grad_middle_norm, grad_gain_two = jax.vjp(normed, middle, gain_second)[1](grad_normal_mid)
    grad_middle = cotangent.astype(jnp.float32) + grad_middle_norm
    grad_branch = grad_middle.astype(jnp.bfloat16)
    (
        conv_whole,
        conv_add,
        proj_whole,
        proj_add,
        gain_one,
        query_whole,
        key_whole,
        value_whole,
        out_whole,
        gain_two,
    ) = (
        lax.all_gather(conv_weight, ("row", "col"), axis=1, tiled=True),
        lax.all_gather(conv_bias, ("row", "col"), axis=0, tiled=True),
        lax.all_gather(proj_weight, ("row", "col"), axis=1, tiled=True),
        lax.all_gather(proj_bias, ("row", "col"), axis=0, tiled=True),
        lax.all_gather(first_gain, ("row", "col"), axis=0, tiled=True),
        lax.all_gather(query_weight, ("row", "col"), axis=0, tiled=True),
        lax.all_gather(key_weight, ("row", "col"), axis=0, tiled=True),
        lax.all_gather(value_weight, ("row", "col"), axis=0, tiled=True),
        lax.all_gather(out_weight, ("row", "col"), axis=1, tiled=True),
        lax.all_gather(second_gain, ("row", "col"), axis=0, tiled=True),
    )
    grad_out = left_contract(mixed, grad_branch)
    grad_mixed = right_contract(grad_branch, out_whole).astype(jnp.bfloat16)
    grad_query, grad_keys, grad_values = lax.map(
        attend_back,
        (
            by_rows(queries),
            by_rows(keys_all),
            by_rows(values_all),
            by_rows(grad_mixed),
            logsum,
            example_rows,
        ),
    )
    grad_query = grad_query.reshape(-1, D).astype(jnp.bfloat16)
    grad_keys = grad_keys.reshape(-1, D).astype(jnp.bfloat16)
    grad_values = grad_values.reshape(-1, D).astype(jnp.bfloat16)
    grad_normal_in = (
        right_contract(grad_query, query_whole)
        + right_contract(grad_keys, key_whole)
        + right_contract(grad_values, value_whole)
    )
    grad_res_norm, grad_gain_one = jax.vjp(normed, residual, gain_first)[1](grad_normal_in)
    grad_residual = grad_middle + grad_res_norm
    pool_width = PATCH_SLOTS + 3 * TEXT
    grad_pooled = jax.vmap(
        lambda chosen, grads: jnp.zeros((pool_width, D), jnp.float32).at[chosen].add(grads)
    )(sources, by_rows(grad_residual))
    grad_arrived = grad_pooled[:, :PATCH_SLOTS].reshape(-1, D).astype(jnp.bfloat16)
    grad_embedded = lax.all_to_all(
        grad_arrived, ("row", "col"), split_axis=0, concat_axis=0, tiled=True
    )
    grad_proj = left_contract(visual, grad_embedded)
    grad_proj_add = jnp.sum(grad_embedded.astype(jnp.float32), axis=0)
    grad_visual = right_contract(grad_embedded, proj_whole).astype(jnp.bfloat16)
    grad_conv = left_contract(patch_rows, grad_visual)
    grad_conv_add = jnp.sum(grad_visual.astype(jnp.float32), axis=0)
    grad_pixels = right_contract(grad_visual, conv_whole).reshape(pixels.shape)
    front_sums = (
        lax.psum_scatter(grad_conv, ("row", "col"), scatter_dimension=1, tiled=True),
        lax.psum_scatter(grad_conv_add, ("row", "col"), scatter_dimension=0, tiled=True),
        lax.psum_scatter(grad_proj, ("row", "col"), scatter_dimension=1, tiled=True),
        lax.psum_scatter(grad_proj_add, ("row", "col"), scatter_dimension=0, tiled=True),
        lax.psum_scatter(grad_gain_one, ("row", "col"), scatter_dimension=0, tiled=True),
        lax.psum_scatter(
            left_contract(normal_in, grad_query), ("row", "col"), scatter_dimension=0, tiled=True
        ),
        lax.psum_scatter(
            left_contract(normal_in, grad_keys), ("row", "col"), scatter_dimension=0, tiled=True
        ),
        lax.psum_scatter(
            left_contract(normal_in, grad_values), ("row", "col"), scatter_dimension=0, tiled=True
        ),
        lax.psum_scatter(grad_out, ("row", "col"), scatter_dimension=1, tiled=True),
        lax.psum_scatter(grad_gain_two, ("row", "col"), scatter_dimension=0, tiled=True),
    )
    return (
        output,
        grad_pixels,
        front_sums[0],
        front_sums[1],
        front_sums[2],
        front_sums[3],
        front_sums[4],
        front_sums[5],
        front_sums[6],
        front_sums[7],
        front_sums[8],
        front_sums[9],
        ffn_sums[0],
        ffn_sums[1],
        ffn_sums[2],
    )


def solution(mesh):
    return jax.shard_map(
        shards,
        mesh=mesh,
        in_specs=(
            P("row", "col", None),
            P(("row", "col"), None),
            P(("row", "col")),
            P(("row", "col")),
            P(("row", "col"), None),
            P(None, ("row", "col")),
            P(("row", "col")),
            P(None, ("row", "col")),
            P(("row", "col")),
            P(("row", "col")),
            P(("row", "col"), None),
            P(("row", "col"), None),
            P(("row", "col"), None),
            P(None, ("row", "col")),
            P(("row", "col")),
            P(("row", "col"), None),
            P(("row", "col"), None),
            P(None, ("row", "col")),
        ),
        out_specs=(
            P(("row", "col"), None),
            P("row", "col", None),
            P(None, ("row", "col")),
            P(("row", "col")),
            P(None, ("row", "col")),
            P(("row", "col")),
            P(("row", "col")),
            P(("row", "col"), None),
            P(("row", "col"), None),
            P(("row", "col"), None),
            P(None, ("row", "col")),
            P(("row", "col")),
            P(("row", "col"), None),
            P(("row", "col"), None),
            P(None, ("row", "col")),
        ),
        check_vma=False,
    )
```

profile of v0, /device:TPU:0, one launch (start us, length us, event | category | flops | bytes accessed | tf_op | source)
XLA Modules:
  0.0 2604.0 jit_solution(6728988985074785193)
XLA Ops:
  16.0 42.4 %all-reduce.10 = (bf16[1024]{0:T(1024)(128)(2,1)S(1)}, bf16[1664]{0:T(1024)(128)(2,1)S(1)}, bf16[1024]{0:T(1024)(128)(2,1)S(1)}, bf16[1024]{0:T(1024)(128)(2,1)S(1)}) all-reduce(bf16[1024]{0:T(1024)(128)(2,1)S(1)} %dynamic-update-slice.1, bf16[1664]{0:T(1024)(128)(2,1)S(1)} %dynamic-update-slice, ...), channel_id=1, replica_groups=mesh['row'=4,'col'=8] {'row','col'}, use_global_device_ids=true, to_apply=%add.1 | all-reduce | flops 4736 | bytes 18944
  58.4 12.4 all-gather.27.cloned.1.call-done
  78.0 54.7 %all-gather.11.cloned.1.call-done = bf16[1664,1024]{0,1:T(8,128)(2,1)} async-done(((bf16[1664,32]{0,1:T(8,128)(2,1)}), bf16[1664,1024]{0,1:T(8,128)(2,1)}) %all-gather.11.cloned.1.call-update) | async-done | bytes 3407888 | tf_op jit(solution)/shard_map/all_gather | solution.py:133
  132.7 8.3 add_convert_fusion.2
  150.5 53.3 %all-to-all-done = bf16[32,32,1024]{2,1,0:T(8,128)(2,1)S(1)} async-done(((bf16[32,32,1024]{2,1,0:T(8,128)(2,1)}), bf16[32,32,1024]{2,1,0:T(8,128)(2,1)S(1)}, u32[]{:S(2)}, u32[]{:S(2)}) %all-to-all-start) | async-done | bytes 2097184 | tf_op jit(solution)/shard_map/all_to_all | solution.py:150
  206.9 21.5 gather_fusion
  247.8 8.9 all-gather.15.cloned.1.call-done
  269.6 45.2 %all-gather.13.cloned.1.call-done = bf16[1024,1024]{1,0:T(8,128)(2,1)} async-done(((bf16[32,1024]{1,0:T(8,128)(2,1)}), bf16[1024,1024]{1,0:T(8,128)(2,1)}) %all-gather.13.cloned.1.call-update) | async-done | bytes 2097168 | tf_op jit(solution)/shard_map/all_gather | solution.py:136
  329.0 151.9 %while.48 = (s32[]{:T(128)}, bf16[16,1152,64]{1,2,0:T(8,128)(2,1)}, f32[16,1152]{1,0:T(8,128)S(1)}, bf16[16,1152,64]{2,1,0:T(8,128)(2,1)}, bf16[16,1152,64]{2,1,...) while((s32[]{:T(128)}, bf16[16,1152,64]{1,2,0:T(8,128)(2,1)}, ...), condition=%wide.region_4.5_spmd.clone, body=%wide.region_1.4_spmd.clone.sunk | while | flops 351681408 | bytes 38412412 | solution.py:63
  490.9 13.3 fusion.89
  511.0 13.0 fusion.90
  524.0 55.9 %all-gather.25.cloned.1.call-done = bf16[2816,1024]{0,1:T(8,128)(2,1)} async-done(((bf16[2816,32]{0,1:T(8,128)(2,1)}), bf16[2816,1024]{0,1:T(8,128)(2,1)}) %all-gather.25.cloned.1.call-update) | async-done | bytes 5767184 | tf_op jit(solution)/shard_map/all_gather | solution.py:145
  579.9 25.6 multiply_convert_fusion.1
  605.5 13.3 fusion.91
  618.9 11.6 multiply_reduce_fusion.1
  649.6 209.3 %while.49 = (s32[]{:T(128)}, bf16[16,1152,64]{1,2,0:T(8,128)(2,1)}, bf16[16,1152,64]{1,2,0:T(8,128)(2,1)}, bf16[16,1152,64]{1,2,0:T(8,128)(2,1)}, bf16[16,1152,6...) while((s32[]{:T(128)}, bf16[16,1152,64]{1,2,0:T(8,128)(2,1)}, ...), condition=%wide.region_9.10_spmd.clone, body=%wide.region_7.9_spmd.clone.sunk | while | flops 862763904 | bytes 42810480 | solution.py:86
  881.4 17.6 scatter_custom_fusion
  902.2 53.0 %all_to_all.18 = bf16[32,32,1024]{2,1,0:T(8,128)(2,1)S(1)} all-to-all(bf16[32,32,1024]{2,1,0:T(8,128)(2,1)S(1)} %bitcast.178), channel_id=1, replica_groups=mesh['row'=4,'col'=8] {'row','col'}, dimensions={0} | all-to-all | bytes 4194304 | tf_op jit(solution)/shard_map/all_to_all | solution.py:257
  996.2 8.0 fusion.93
  1004.3 13.6 fusion.94
  1018.4 13.5 fusion.95
  1031.9 13.7 fusion.96
  1045.7 13.3 add_convert_fusion.1
  1063.7 38.9 %all-reduce.9 = (f32[1664]{0:T(1024)S(1)}, f32[1024]{0:T(1024)S(1)}, f32[1024]{0:T(1024)S(1)}, f32[1024]{0:T(1024)S(1)}) all-reduce(f32[1664]{0:T(1024)S(1)} %get-tuple-element.307, f32[1024]{0:T(1024)S(1)} %convert_reduce_fusion.1, f32[1024]{0:T(1024)S(1)} %get-tuple-element.250, ...), channel_id=3, replica_groups=mesh['row'=4,'col'=8] {'row','col'}, use_global_device_ids=true, to_apply=%region_14.15.clone | all-reduce | flops 4736 | bytes 37888
  1114.1 138.6 %reduce-scatter.12.cloned.1.call-done = f32[32,1024]{1,0:T(8,128)} async-done(((f32[1024,1024]{1,0:T(8,128)}), f32[32,1024]{1,0:T(8,128)}) %reduce-scatter.12.cloned.1.call-update) | async-done | bytes 131088 | tf_op jit(solution)/shard_map/reduce_scatter | solution.py:272
  1252.7 145.2 %reduce-scatter.14.cloned.1.call-done = f32[32,1024]{1,0:T(8,128)} async-done(((f32[1024,1024]{1,0:T(8,128)}), f32[32,1024]{1,0:T(8,128)}) %reduce-scatter.14.cloned.1.call-update) | async-done | bytes 131088 | tf_op jit(solution)/shard_map/reduce_scatter | solution.py:275
  1397.9 144.6 %reduce-scatter.16.cloned.1.call-done = f32[32,1024]{1,0:T(8,128)} async-done(((f32[1024,1024]{1,0:T(8,128)}), f32[32,1024]{1,0:T(8,128)}) %reduce-scatter.16.cloned.1.call-update) | async-done | bytes 131088 | tf_op jit(solution)/shard_map/reduce_scatter | solution.py:278
  1542.5 145.0 %reduce-scatter.18.cloned.1.call-done = f32[1024,32]{0,1:T(8,128)} async-done(((f32[1024,1024]{0,1:T(8,128)}), f32[1024,32]{0,1:T(8,128)}) %reduce-scatter.18.cloned.1.call-update) | async-done | bytes 131088 | tf_op jit(solution)/shard_map/reduce_scatter | solution.py:281
  1687.5 155.7 %reduce-scatter.10.cloned.1.call-done = f32[1664,32]{0,1:T(8,128)} async-done(((f32[1664,1024]{0,1:T(8,128)}), f32[1664,32]{0,1:T(8,128)}) %reduce-scatter.10.cloned.1.call-update) | async-done | bytes 213008 | tf_op jit(solution)/shard_map/reduce_scatter | solution.py:269
  1843.2 251.7 %reduce-scatter.20.cloned.1.call-done = f32[32,2816]{1,0:T(8,128)} async-done(((f32[1024,2816]{1,0:T(8,128)}), f32[32,2816]{1,0:T(8,128)}) %reduce-scatter.20.cloned.1.call-update) | async-done | bytes 360464 | tf_op jit(solution)/shard_map/reduce_scatter | solution.py:194
  2095.0 250.7 %reduce-scatter.22.cloned.1.call-done = f32[32,2816]{1,0:T(8,128)} async-done(((f32[1024,2816]{1,0:T(8,128)}), f32[32,2816]{1,0:T(8,128)}) %reduce-scatter.22.cloned.1.call-update) | async-done | bytes 360464 | tf_op jit(solution)/shard_map/reduce_scatter | solution.py:197
  2345.7 251.2 %reduce-scatter.24.cloned.1.call-done = f32[2816,32]{0,1:T(8,128)} async-done(((f32[2816,1024]{0,1:T(8,128)}), f32[2816,32]{0,1:T(8,128)}) %reduce-scatter.24.cloned.1.call-update) | async-done | bytes 360464 | tf_op jit(solution)/shard_map/reduce_scatter | solution.py:200
  (405 shorter events, 553.9 us)
Async XLA Ops:
  7.2 66.4 %copy-start = (bf16[32,32,588]{2,1,0:T(8,128)(2,1)S(1)}, bf16[32,32,588]{2,1,0:T(8,128)(2,1)}, u32[]{:S(2)}) copy-start(bf16[32,32,588]{2,1,0:T(8,128)(2,1)} %param.22) | copy-start | bytes 3612676
  7.2 63.6 %all-gather.27.cloned.1.call-start = ((), (), s32[]{:S(2)}) async-start(), calls=%async_computation.26 | async-start | bytes 2365440 | tf_op jit(solution)/shard_map/all_gather | solution.py:131
  7.9 124.8 %all-gather.11.cloned.1.call-start = ((), (), s32[]{:S(2)}) async-start(), calls=%async_computation.10 | async-start | bytes 3514368 | tf_op jit(solution)/shard_map/all_gather | solution.py:133
  8.7 226.7 %all-gather.17.cloned.1.call-start = ((), (), s32[]{:S(2)}) async-start(), calls=%async_computation.13 | async-start | bytes 2162688 | tf_op jit(solution)/shard_map/all_gather | solution.py:138
  9.4 247.3 %all-gather.15.cloned.1.call-start = ((), (), s32[]{:S(2)}) async-start(), calls=%async_computation.12 | async-start | bytes 2162688 | tf_op jit(solution)/shard_map/all_gather | solution.py:137
  10.0 304.9 %all-gather.13.cloned.1.call-start = ((), (), s32[]{:S(2)}) async-start(), calls=%async_computation.11 | async-start | bytes 2162688 | tf_op jit(solution)/shard_map/all_gather | solution.py:136
  10.6 470.3 %all-gather.19.cloned.1.call-start = ((), (), s32[]{:S(2)}) async-start(), calls=%async_computation.14 | async-start | bytes 2162688 | tf_op jit(solution)/shard_map/all_gather | solution.py:139
  11.2 479.7 %all-gather.21.cloned.1.call-start = ((), (), s32[]{:S(2)}) async-start(), calls=%async_computation.15 | async-start | bytes 5947392 | tf_op jit(solution)/shard_map/all_gather | solution.py:143
  11.9 499.1 %all-gather.23.cloned.1.call-start = ((), (), s32[]{:S(2)}) async-start(), calls=%async_computation.16 | async-start | bytes 5947392 | tf_op jit(solution)/shard_map/all_gather | solution.py:144
  78.0 67.2 %copy-start.15 = (s32[1152]{0:T(1024)S(1)}, s32[1152]{0:T(1024)}, u32[]{:S(2)}) copy-start(s32[1152]{0:T(1024)} %param.24) | copy-start | bytes 13828
  141.0 8.7 copy-start.18
  141.0 8.7 copy-start.17
  141.0 62.8 %all-to-all-start = ((bf16[32,32,1024]{2,1,0:T(8,128)(2,1)}), bf16[32,32,1024]{2,1,0:T(8,128)(2,1)S(1)}, u32[]{:S(2)}, u32[]{:S(2)}) async-start(bf16[32,32,1024]{2,1,0:T(8,128)(2,1)} %bitcast.191), calls=%async_computation | async-start | bytes 4194304 | tf_op jit(solution)/shard_map/all_to_all | solution.py:150
  144.2 435.7 %all-gather.25.cloned.1.call-start = ((), (), s32[]{:S(2)}) async-start(), calls=%async_computation.17 | async-start | bytes 5947392 | tf_op jit(solution)/shard_map/all_gather | solution.py:145
  144.9 967.1 %all-reduce.13.cloned.1.call-start = ((), (), s32[]{:S(2)}) async-start(), calls=%async_computation.27 | async-start | bytes 7880704
  145.3 169.5 %copy-start.13 = (f32[1024]{0:T(1024)}, f32[1024]{0:T(1024)S(1)}, u32[]{:S(2)}) copy-start(f32[1024]{0:T(1024)S(1)} %convert_element_type.168) | copy-start | bytes 12292
  235.4 79.4 %copy-start.11 = (f32[1152]{0:T(1024)}, f32[1152]{0:T(1024)S(1)}, u32[]{:S(2)}) copy-start(f32[1152]{0:T(1024)S(1)} %fusion.73) | copy-start | bytes 13828
  321.7 7.3 copy-start.8
  605.5 13.3 copy-start.19
  605.5 13.3 copy-start.26
  618.9 11.7 copy-start.5
  649.6 209.3 %copy-start.22 = (bf16[1024,1024]{1,0:T(8,128)(2,1)S(1)}, bf16[1024,1024]{1,0:T(8,128)(2,1)}, u32[]{:S(2)}) copy-start(bf16[1024,1024]{1,0:T(8,128)(2,1)} %all-gather.15.cloned.1.call-done) | copy-start | bytes 6291460
  863.7 8.3 slice-start
  902.0 53.2 %copy-start.20 = (bf16[1664,1024]{0,1:T(8,128)(2,1)S(1)}, bf16[1664,1024]{0,1:T(8,128)(2,1)}, u32[]{:S(2)}) copy-start(bf16[1664,1024]{0,1:T(8,128)(2,1)} %all-gather.11.cloned.1.call-done) | copy-start | bytes 10223620
  965.5 287.2 %reduce-scatter.12.cloned.1.call-start = ((), (), s32[]{:S(2)}) async-start(), calls=%async_computation.19 | async-start | bytes 4325376 | tf_op jit(solution)/shard_map/reduce_scatter | solution.py:272
  972.8 425.2 %reduce-scatter.14.cloned.1.call-start = ((), (), s32[]{:S(2)}) async-start(), calls=%async_computation.20 | async-start | bytes 4325376 | tf_op jit(solution)/shard_map/reduce_scatter | solution.py:275
  980.5 562.0 %reduce-scatter.16.cloned.1.call-start = ((), (), s32[]{:S(2)}) async-start(), calls=%async_computation.21 | async-start | bytes 4325376 | tf_op jit(solution)/shard_map/reduce_scatter | solution.py:278
  988.1 699.4 %reduce-scatter.18.cloned.1.call-start = ((), (), s32[]{:S(2)}) async-start(), calls=%async_computation.22 | async-start | bytes 4325376 | tf_op jit(solution)/shard_map/reduce_scatter | solution.py:281
  996.2 847.1 %reduce-scatter.10.cloned.1.call-start = ((), (), s32[]{:S(2)}) async-start(), calls=%async_computation.18 | async-start | bytes 7028736 | tf_op jit(solution)/shard_map/reduce_scatter | solution.py:269
  1004.2 1090.7 %reduce-scatter.20.cloned.1.call-start = ((), (), s32[]{:S(2)}) async-start(), calls=%async_computation.23 | async-start | bytes 11894784 | tf_op jit(solution)/shard_map/reduce_scatter | solution.py:194
  1017.9 1327.8 %reduce-scatter.22.cloned.1.call-start = ((), (), s32[]{:S(2)}) async-start(), calls=%async_computation.24 | async-start | bytes 11894784 | tf_op jit(solution)/shard_map/reduce_scatter | solution.py:197
  1031.9 1565.0 %reduce-scatter.24.cloned.1.call-start = ((), (), s32[]{:S(2)}) async-start(), calls=%async_computation.25 | async-start | bytes 11894784 | tf_op jit(solution)/shard_map/reduce_scatter | solution.py:200
  (31 other events, 90.3 us)
Sparse Core Ops, SparseCore 0:
  11.0 59.7 all-gather.26
  73.7 58.9 all-gather.10
  135.7 62.8 all-gather.16
  201.4 55.3 all-gather.14
  259.6 55.2 all-gather.12
  317.7 55.2 all-gather.18
  375.9 66.1 all-gather.20
  445.0 65.9 all-gather.22
  513.9 65.9 all-gather.24
  965.6 139.5 all-reduce.12
  1108.1 144.5 reduce-scatter.11
  1255.4 142.4 reduce-scatter.13
  1400.8 141.7 reduce-scatter.15
  1545.2 142.2 reduce-scatter.17
  1690.2 152.9 reduce-scatter.9
  1846.0 248.9 reduce-scatter.19
  2097.7 247.9 reduce-scatter.21
  2348.4 248.4 reduce-scatter.23
where the time goes:
time: 2610 us; the launch traced here: 2600 us
  waiting for transfers between devices  1730 us (66%)
  matrix products  539 us (21%)
  blocking collectives  134 us (5%)
  local copies, waits for them, and re-layouts  124 us (5%)
  other arithmetic  59.7 us (2%)
    reduce_scatter x1, waiting for transfers between devices, shards(): lax.psum_scatter(left_contract(normal_mid, grad_gate), ('row', 'col'), sc...  252 us
    reduce_scatter x1, waiting for transfers between devices, shards(): lax.psum_scatter(grad_down, ('row', 'col'), scatter_dimension=1, tiled=True)  251 us
    reduce_scatter x1, waiting for transfers between devices, shards(): lax.psum_scatter(left_contract(normal_mid, grad_upward), ('row', 'col'),...  251 us
    dot_general x57, matrix products, right_contract(): lax.dot_general(left, right, (((1,), (1,)), ((), ())), preferred_element_...  191 us
    dot_general x41, matrix products, matmul(): return jnp.dot(left, right, preferred_element_type=jnp.float32)  183 us
    dot_general x41, matrix products, left_contract(): lax.dot_general(left, right, (((0,), (0,)), ((), ())), preferred_element_...  165 us
    reduce_scatter x1, waiting for transfers between devices, shards(): lax.psum_scatter(grad_proj, ('row', 'col'), scatter_dimension=1, tiled=True)  156 us
    reduce_scatter x1, waiting for transfers between devices, shards(): lax.psum_scatter(left_contract(normal_in, grad_keys), ('row', 'col'), sca...  145 us
  transfers between devices with their start and end apart: 19, of which 15 were waited for; matrix products, arithmetic and copies ran while one was open for 14% of the time, Pallas kernels for 0%

commit v1 on v0

--- a/solution.py
+++ b/solution.py
@@ -9,6 +9,18 @@
 PATCH_SLOTS = 1024
 TEXT = 128
 ROW = 1152
+
+
+def gather_by_bits(x, axis, dim):
+    ways, here, step = (lax.axis_size(axis), lax.axis_index(axis), x.shape[dim])
+    line, have = (x, 1)
+    while have < ways:
+        line = jnp.concatenate(
+            [line, lax.ppermute(line, axis, [(d, (d - have) % ways) for d in range(ways)])],
+            axis=dim,
+        )
+        have = 2 * have
+    return jnp.roll(line, here * step, axis=dim)
 
 
 def normed(values, gain):
@@ -130,7 +142,7 @@
     ) = (
         lax.all_gather(conv_weight, ("row", "col"), axis=1, tiled=True),
         lax.all_gather(conv_bias, ("row", "col"), axis=0, tiled=True),
-        lax.all_gather(proj_weight, ("row", "col"), axis=1, tiled=True),
+        gather_by_bits(proj_weight, ("row", "col"), 1),
         lax.all_gather(proj_bias, ("row", "col"), axis=0, tiled=True),
         lax.all_gather(first_gain, ("row", "col"), axis=0, tiled=True),
         lax.all_gather(query_weight, ("row", "col"), axis=0, tiled=True),

time: 2610 us -> 2570 us (0.985)
  waiting for transfers between devices: 1730 us -> 1670 us
    all_gather x1, waiting for transfers between devices: 54.7 us -> 0.02 us  [shards(): lax.all_gather(proj_weight, ('row', 'col'), axis=1, tiled=True)]
    all_to_all x1 -> x0, blocking collectives: 53 us -> none  [shards(): lax.all_to_all(grad_arrived, ('row', 'col'), split_axis=0, concat_axis=0,...]
    all_to_all x0 -> x1, waiting for transfers between devices: none -> 49.9 us  [shards(): lax.all_to_all(grad_arrived, ('row', 'col'), split_axis=0, concat_axis=0,...]
    all_gather x1, waiting for transfers between devices: 45.2 us -> 0.02 us  [shards(): lax.all_gather(query_weight, ('row', 'col'), axis=0, tiled=True)]
    ppermute x0 -> x5, waiting for transfers between devices: none -> 42.3 us  [gather_by_bits(): lax.ppermute(line, axis, [(d, (d - have) % ways) for d in range(ways)])]
    unnamed x2, blocking collectives: 81.3 us -> 111 us
  transfers between devices with their start and end apart: 19 -> 25, of which waited for: 15 -> 15; matrix products, arithmetic and copies ran while one was open for 14% -> 27% of each run, Pallas kernels for 0% -> 0%
where the time goes in v1:
time: 2570 us; the launch traced here: 2560 us
  waiting for transfers between devices  1670 us (65%)
  matrix products  536 us (21%)
  local copies, waits for them, and re-layouts  141 us (5%)
  blocking collectives  111 us (4%)
  other arithmetic  64.8 us (3%)
    reduce_scatter x1, waiting for transfers between devices, shards(): lax.psum_scatter(left_contract(normal_mid, grad_gate), ('row', 'col'), sc...  252 us
    reduce_scatter x1, waiting for transfers between devices, shards(): lax.psum_scatter(grad_down, ('row', 'col'), scatter_dimension=1, tiled=True)  251 us
    reduce_scatter x1, waiting for transfers between devices, shards(): lax.psum_scatter(left_contract(normal_mid, grad_upward), ('row', 'col'),...  250 us
    dot_general x57, matrix products, right_contract(): lax.dot_general(left, right, (((1,), (1,)), ((), ())), preferred_element_...  193 us
    dot_general x41, matrix products, matmul(): return jnp.dot(left, right, preferred_element_type=jnp.float32)  178 us
    dot_general x41, matrix products, left_contract(): lax.dot_general(left, right, (((0,), (0,)), ((), ())), preferred_element_...  165 us
    reduce_scatter x1, waiting for transfers between devices, shards(): lax.psum_scatter(grad_proj, ('row', 'col'), scatter_dimension=1, tiled=True)  155 us
    reduce_scatter x1, waiting for transfers between devices, shards(): lax.psum_scatter(left_contract(normal_in, grad_values), ('row', 'col'), s...  145 us
  transfers between devices with their start and end apart: 25, of which 15 were waited for; matrix products, arithmetic and copies ran while one was open for 27% of the time, Pallas kernels for 0%

profile of v1, /device:TPU:0, one launch (start us, length us, event | category | flops | bytes accessed | tf_op | source)
XLA Modules:
  0.0 2560.2 jit_solution(16019986434787524089)
XLA Ops:
  31.1 22.8 collective-permute-done.2
  61.6 10.1 collective-permute-done.3
  77.0 73.1 %all-reduce.10 = (bf16[1024]{0:T(1024)(128)(2,1)}, bf16[1664]{0:T(1024)(128)(2,1)}, bf16[1024]{0:T(1024)(128)(2,1)}, bf16[1024]{0:T(1024)(128)(2,1)}) all-reduce(bf16[1024]{0:T(1024)(128)(2,1)} %copy-done.20, bf16[1664]{0:T(1024)(128)(2,1)S(1)} %dynamic-update-slice, ...), channel_id=1, replica_groups=mesh['row'=4,'col'=8] {'row','col'}, use_global_device_ids=true, to_apply=%add.1 | all-reduce | flops 4736 | bytes 18944
  182.3 50.9 %all-to-all-done = bf16[32,32,1024]{2,1,0:T(8,128)(2,1)S(1)} async-done(((bf16[32,32,1024]{2,1,0:T(8,128)(2,1)}), bf16[32,32,1024]{2,1,0:T(8,128)(2,1)S(1)}, u32[]{:S(2)}, u32[]{:S(2)}) %all-to-all-start) | async-done | bytes 2097184 | tf_op jit(solution)/shard_map/all_to_all | solution.py:162
  236.3 21.4 gather_fusion
  304.3 152.1 %while.48 = (s32[]{:T(128)}, bf16[16,1152,64]{1,2,0:T(8,128)(2,1)}, f32[16,1152]{1,0:T(8,128)S(1)}, bf16[16,1152,64]{2,1,0:T(8,128)(2,1)}, bf16[16,1152,64]{2,1,...) while((s32[]{:T(128)}, bf16[16,1152,64]{1,2,0:T(8,128)(2,1)}, ...), condition=%wide.region_4.5_spmd.clone, body=%wide.region_1.4_spmd.clone.sunk | while | flops 351681408 | bytes 38412412 | solution.py:75
  466.4 13.2 fusion.94
  479.6 13.0 fusion.95
  492.7 40.6 %all-gather.23.cloned.1.call-done = bf16[2816,1024]{0,1:T(8,128)(2,1)} async-done(((bf16[2816,32]{0,1:T(8,128)(2,1)}), bf16[2816,1024]{0,1:T(8,128)(2,1)}) %all-gather.23.cloned.1.call-update) | async-done | bytes 5767184 | tf_op jit(solution)/shard_map/all_gather | solution.py:157
  533.3 25.5 multiply_convert_fusion.1
  558.9 13.4 fusion.96
  572.3 11.6 multiply_reduce_fusion.1
  602.9 209.3 %while.49 = (s32[]{:T(128)}, bf16[16,1152,64]{1,2,0:T(8,128)(2,1)}, bf16[16,1152,64]{1,2,0:T(8,128)(2,1)}, bf16[16,1152,64]{1,2,0:T(8,128)(2,1)}, bf16[16,1152,6...) while((s32[]{:T(128)}, bf16[16,1152,64]{1,2,0:T(8,128)(2,1)}, ...), condition=%wide.region_9.10_spmd.clone, body=%wide.region_7.9_spmd.clone.sunk | while | flops 862763904 | bytes 42810480 | solution.py:98
  834.9 17.7 scatter_custom_fusion
  860.6 49.9 %all-to-all-done.1 = bf16[32,32,1024]{2,1,0:T(8,128)(2,1)S(1)} async-done(((bf16[32,32,1024]{2,1,0:T(8,128)(2,1)}), bf16[32,32,1024]{2,1,0:T(8,128)(2,1)S(1)}, u32[]{:S(2)}, u32[]{:S(2)}) %all-to-all-start.1) | async-done | bytes 2097184 | tf_op jit(solution)/shard_map/all_to_all | solution.py:269
  922.8 7.9 fusion.73
  931.0 7.5 fusion.84
  938.6 7.4 fusion.86
  953.5 8.0 fusion.98
  961.5 13.6 fusion.100
  975.6 13.6 fusion.99
  989.2 13.6 fusion.101
  1002.9 13.3 add_convert_fusion.1
  1020.9 38.0 %all-reduce.9 = (f32[1664]{0:T(1024)S(1)}, f32[1024]{0:T(1024)S(1)}, f32[1024]{0:T(1024)S(1)}, f32[1024]{0:T(1024)S(1)}) all-reduce(f32[1664]{0:T(1024)S(1)} %get-tuple-element.317, f32[1024]{0:T(1024)S(1)} %convert_reduce_fusion.1, f32[1024]{0:T(1024)S(1)} %get-tuple-element.250, ...), channel_id=3, replica_groups=mesh['row'=4,'col'=8] {'row','col'}, use_global_device_ids=true, to_apply=%region_14.15.clone | all-reduce | flops 4736 | bytes 37888
  1070.4 139.7 %reduce-scatter.18.cloned.1.call-done = f32[1024,32]{0,1:T(8,128)} async-done(((f32[1024,1024]{0,1:T(8,128)}), f32[1024,32]{0,1:T(8,128)}) %reduce-scatter.18.cloned.1.call-update) | async-done | bytes 131088 | tf_op jit(solution)/shard_map/reduce_scatter | solution.py:293
  1210.1 145.1 %reduce-scatter.16.cloned.1.call-done = f32[32,1024]{1,0:T(8,128)} async-done(((f32[1024,1024]{1,0:T(8,128)}), f32[32,1024]{1,0:T(8,128)}) %reduce-scatter.16.cloned.1.call-update) | async-done | bytes 131088 | tf_op jit(solution)/shard_map/reduce_scatter | solution.py:290
  1355.2 145.0 %reduce-scatter.14.cloned.1.call-done = f32[32,1024]{1,0:T(8,128)} async-done(((f32[1024,1024]{1,0:T(8,128)}), f32[32,1024]{1,0:T(8,128)}) %reduce-scatter.14.cloned.1.call-update) | async-done | bytes 131088 | tf_op jit(solution)/shard_map/reduce_scatter | solution.py:287
  1500.2 144.4 %reduce-scatter.12.cloned.1.call-done = f32[32,1024]{1,0:T(8,128)} async-done(((f32[1024,1024]{1,0:T(8,128)}), f32[32,1024]{1,0:T(8,128)}) %reduce-scatter.12.cloned.1.call-update) | async-done | bytes 131088 | tf_op jit(solution)/shard_map/reduce_scatter | solution.py:284
  1644.5 155.4 %reduce-scatter.10.cloned.1.call-done = f32[1664,32]{0,1:T(8,128)} async-done(((f32[1664,1024]{0,1:T(8,128)}), f32[1664,32]{0,1:T(8,128)}) %reduce-scatter.10.cloned.1.call-update) | async-done | bytes 213008 | tf_op jit(solution)/shard_map/reduce_scatter | solution.py:281
  1799.9 249.8 %reduce-scatter.22.cloned.1.call-done = f32[32,2816]{1,0:T(8,128)} async-done(((f32[1024,2816]{1,0:T(8,128)}), f32[32,2816]{1,0:T(8,128)}) %reduce-scatter.22.cloned.1.call-update) | async-done | bytes 360464 | tf_op jit(solution)/shard_map/reduce_scatter | solution.py:209
  2049.8 252.1 %reduce-scatter.20.cloned.1.call-done = f32[32,2816]{1,0:T(8,128)} async-done(((f32[1024,2816]{1,0:T(8,128)}), f32[32,2816]{1,0:T(8,128)}) %reduce-scatter.20.cloned.1.call-update) | async-done | bytes 360464 | tf_op jit(solution)/shard_map/reduce_scatter | solution.py:206
  2301.9 251.2 %reduce-scatter.24.cloned.1.call-done = f32[2816,32]{0,1:T(8,128)} async-done(((f32[2816,1024]{0,1:T(8,128)}), f32[2816,32]{0,1:T(8,128)}) %reduce-scatter.24.cloned.1.call-update) | async-done | bytes 360464 | tf_op jit(solution)/shard_map/reduce_scatter | solution.py:212
  (453 shorter events, 574.8 us)
Async XLA Ops:
  7.2 155.9 %copy-start = (bf16[32,32,588]{2,1,0:T(8,128)(2,1)S(1)}, bf16[32,32,588]{2,1,0:T(8,128)(2,1)}, u32[]{:S(2)}) copy-start(bf16[32,32,588]{2,1,0:T(8,128)(2,1)} %param.22) | copy-start | bytes 3612676
  7.2 65.9 %copy-start.34 = (bf16[32]{0:T(256)(128)(2,1)S(1)}, bf16[32]{0:T(256)(128)(2,1)}, u32[]{:S(2)}) copy-start(bf16[32]{0:T(256)(128)(2,1)} %param.30) | copy-start | bytes 196
  7.2 153.1 %all-gather.27.cloned.1.call-start = ((), (), s32[]{:S(2)}) async-start(), calls=%async_computation.26 | async-start | bytes 2365440 | tf_op jit(solution)/shard_map/all_gather | solution.py:143
  7.9 256.9 %all-gather.15.cloned.1.call-start = ((), (), s32[]{:S(2)}) async-start(), calls=%async_computation.12 | async-start | bytes 2162688 | tf_op jit(solution)/shard_map/all_gather | solution.py:150
  8.7 268.6 %all-gather.13.cloned.1.call-start = ((), (), s32[]{:S(2)}) async-start(), calls=%async_computation.11 | async-start | bytes 2162688 | tf_op jit(solution)/shard_map/all_gather | solution.py:149
  9.4 280.8 %all-gather.11.cloned.1.call-start = ((), (), s32[]{:S(2)}) async-start(), calls=%async_computation.10 | async-start | bytes 2162688 | tf_op jit(solution)/shard_map/all_gather | solution.py:148
  10.0 446.4 %all-gather.17.cloned.1.call-start = ((), (), s32[]{:S(2)}) async-start(), calls=%async_computation.13 | async-start | bytes 2162688 | tf_op jit(solution)/shard_map/all_gather | solution.py:151
  10.6 455.9 %all-gather.19.cloned.1.call-start = ((), (), s32[]{:S(2)}) async-start(), calls=%async_computation.14 | async-start | bytes 5947392 | tf_op jit(solution)/shard_map/all_gather | solution.py:155
  11.2 468.5 %all-gather.21.cloned.1.call-start = ((), (), s32[]{:S(2)}) async-start(), calls=%async_computation.15 | async-start | bytes 5947392 | tf_op jit(solution)/shard_map/all_gather | solution.py:156
  11.9 521.4 %all-gather.23.cloned.1.call-start = ((), (), s32[]{:S(2)}) async-start(), calls=%async_computation.16 | async-start | bytes 5947392 | tf_op jit(solution)/shard_map/all_gather | solution.py:157
  12.7 9.2 collective-permute-start
  21.8 51.3 %copy-start.10 = (bf16[1664,32]{0,1:T(8,128)(2,1)}, bf16[1664,32]{0,1:T(8,128)(2,1)S(1)}, u32[]{:S(2)}) copy-start(bf16[1664,32]{0,1:T(8,128)(2,1)S(1)} %collective-permute-done) | copy-start | bytes 319492
  22.8 7.2 collective-permute-start.1
  30.0 43.1 %copy-start.9 = (bf16[1664,64]{0,1:T(8,128)(2,1)}, bf16[1664,64]{0,1:T(8,128)(2,1)S(1)}, u32[]{:S(2)}) copy-start(bf16[1664,64]{0,1:T(8,128)(2,1)S(1)} %collective-permute-done.1) | copy-start | bytes 638980
  31.0 22.9 collective-permute-start.2
  54.9 98.5 %copy-start.6 = (bf16[1664,32]{0,1:T(8,128)(2,1)S(1)}, bf16[1664,32]{0,1:T(8,128)(2,1)}, u32[]{:S(2)}) copy-start(bf16[1664,32]{0,1:T(8,128)(2,1)} %param.29) | copy-start | bytes 319492
  54.9 16.8 collective-permute-start.3
  73.1 79.0 %collective-permute-start.4 = (bf16[1664,512]{0,1:T(8,128)(2,1)}, bf16[1664,512]{0,1:T(8,128)(2,1)S(1)}, u32[]{:S(2)}, u32[]{:S(2)}) collective-permute-start(bf16[1664,512]{0,1:T(8,128)(2,1)} %get-tuple-element.301), channel_id=1, source_target_pairs={{0,16},{1,17},{2,18},{3,19},{4,20},{5,21},{6,22},{7,23},{8,24},{9,... | collective-permute-start | bytes 5111816 | tf_op jit(solution)/shard_map/ppermute | solution.py:19
  172.1 61.2 %all-to-all-start = ((bf16[32,32,1024]{2,1,0:T(8,128)(2,1)}), bf16[32,32,1024]{2,1,0:T(8,128)(2,1)S(1)}, u32[]{:S(2)}, u32[]{:S(2)}) async-start(bf16[32,32,1024]{2,1,0:T(8,128)(2,1)} %bitcast.190), calls=%async_computation | async-start | bytes 4194304 | tf_op jit(solution)/shard_map/all_to_all | solution.py:162
  176.3 684.3 %all-gather.25.cloned.1.call-start = ((), (), s32[]{:S(2)}) async-start(), calls=%async_computation.17 | async-start | bytes 3514368 | tf_op jit(solution)/shard_map/all_gather | solution.py:232
  177.1 113.1 %copy-start.18 = (f32[1024]{0:T(1024)}, f32[1024]{0:T(1024)S(1)}, u32[]{:S(2)}) copy-start(f32[1024]{0:T(1024)S(1)} %convert_element_type.168) | copy-start | bytes 12292
  602.9 209.3 %copy-start.31 = (bf16[1024,1024]{1,0:T(8,128)(2,1)S(1)}, bf16[1024,1024]{1,0:T(8,128)(2,1)}, u32[]{:S(2)}) copy-start(bf16[1024,1024]{1,0:T(8,128)(2,1)} %all-gather.13.cloned.1.call-done) | copy-start | bytes 6291460
  857.2 53.2 %all-to-all-start.1 = ((bf16[32,32,1024]{2,1,0:T(8,128)(2,1)}), bf16[32,32,1024]{2,1,0:T(8,128)(2,1)S(1)}, u32[]{:S(2)}, u32[]{:S(2)}) async-start(bf16[32,32,1024]{2,1,0:T(8,128)(2,1)} %bitcast.177), calls=%async_computation.1 | async-start | bytes 4194304 | tf_op jit(solution)/shard_map/all_to_all | solution.py:269
  860.5 207.9 %all-reduce.13.cloned.1.call-start = ((), (), s32[]{:S(2)}) async-start(), calls=%async_computation.27 | async-start | bytes 7880704
  922.8 287.3 %reduce-scatter.18.cloned.1.call-start = ((), (), s32[]{:S(2)}) async-start(), calls=%async_computation.22 | async-start | bytes 4325376 | tf_op jit(solution)/shard_map/reduce_scatter | solution.py:293
  930.8 424.4 %reduce-scatter.16.cloned.1.call-start = ((), (), s32[]{:S(2)}) async-start(), calls=%async_computation.21 | async-start | bytes 4325376 | tf_op jit(solution)/shard_map/reduce_scatter | solution.py:290
  938.5 561.6 %reduce-scatter.14.cloned.1.call-start = ((), (), s32[]{:S(2)}) async-start(), calls=%async_computation.20 | async-start | bytes 4325376 | tf_op jit(solution)/shard_map/reduce_scatter | solution.py:287
  946.0 698.5 %reduce-scatter.12.cloned.1.call-start = ((), (), s32[]{:S(2)}) async-start(), calls=%async_computation.19 | async-start | bytes 4325376 | tf_op jit(solution)/shard_map/reduce_scatter | solution.py:284
  953.4 846.5 %reduce-scatter.10.cloned.1.call-start = ((), (), s32[]{:S(2)}) async-start(), calls=%async_computation.18 | async-start | bytes 7028736 | tf_op jit(solution)/shard_map/reduce_scatter | solution.py:281
  961.5 1088.3 %reduce-scatter.22.cloned.1.call-start = ((), (), s32[]{:S(2)}) async-start(), calls=%async_computation.24 | async-start | bytes 11894784 | tf_op jit(solution)/shard_map/reduce_scatter | solution.py:209
  975.1 1326.7 %reduce-scatter.20.cloned.1.call-start = ((), (), s32[]{:S(2)}) async-start(), calls=%async_computation.23 | async-start | bytes 11894784 | tf_op jit(solution)/shard_map/reduce_scatter | solution.py:206
  989.2 1563.9 %reduce-scatter.24.cloned.1.call-start = ((), (), s32[]{:S(2)}) async-start(), calls=%async_computation.25 | async-start | bytes 11894784 | tf_op jit(solution)/shard_map/reduce_scatter | solution.py:212
  (48 other events, 240.8 us)
Sparse Core Ops, SparseCore 0:
  11.0 70.9 all-gather.26
  85.0 56.3 all-gather.14
  144.3 66.1 all-gather.12
  213.3 55.0 all-gather.10
  271.3 55.2 all-gather.16
  329.3 66.1 all-gather.18
  398.4 65.9 all-gather.20
  467.3 65.9 all-gather.22
  536.2 58.7 all-gather.24
  922.9 140.1 all-reduce.12
  1066.0 144.0 reduce-scatter.17
  1212.8 142.3 reduce-scatter.15
  1358.0 142.0 reduce-scatter.13
  1502.9 141.6 reduce-scatter.11
  1647.3 152.6 reduce-scatter.9
  1802.7 247.0 reduce-scatter.21
  2052.5 249.3 reduce-scatter.19
  2304.6 248.4 reduce-scatter.23
